TPU v7x, 32 devices: a whole 2x2x4 slice. The times are simulated.
32 devices in a mesh: dp: 4 (over x, core), fsdp: 8 (over z, y).
Axes of the slice: x: 2, y: 2, z: 4, core: 2. Of those that a mesh axis runs over, the one named last changes fastest.
Arguments:
- tokens: bfloat16 [32768, 768], P(('dp', 'fsdp')), may hold values from -6 to 6
- segment_ids: int32 [64, 512], P(('dp', 'fsdp')), may hold values from 0 to 7, never falling along the last dimension, each value on 1 to 160 neighbouring positions
- query_weight: bfloat16 [768, 768], P('fsdp'), may hold values from -0.21875 to 0.21875
- query_bias: bfloat16 [768], P('fsdp'), may hold values from -3 to 3
- key_weight: bfloat16 [768, 768], P('fsdp'), may hold values from -0.21875 to 0.21875
- value_weight: bfloat16 [768, 768], P('fsdp'), may hold values from -0.21875 to 0.21875
- value_bias: bfloat16 [768], P('fsdp'), may hold values from -3 to 3
- out_weight: bfloat16 [768, 768], P('fsdp'), may hold values from -0.625 to 0.625
- out_bias: bfloat16 [768], P('fsdp'), may hold values from -3 to 3
- first_gain: bfloat16 [768], P('fsdp'), may hold values from 0.25 to 1.75
- first_shift: bfloat16 [768], P('fsdp'), may hold values from -3 to 3
- expand_weight: bfloat16 [768, 3072], P('fsdp'), may hold values from -0.21875 to 0.21875
- expand_bias: bfloat16 [3072], P('fsdp'), may hold values from -3 to 3
- reduce_weight: bfloat16 [3072, 768], P('fsdp'), may hold values from -0.109375 to 0.109375
- reduce_bias: bfloat16 [768], P('fsdp'), may hold values from -3 to 3
- second_gain: bfloat16 [768], P('fsdp'), may hold values from 0.25 to 1.75
- second_shift: bfloat16 [768], P('fsdp'), may hold values from -3 to 3
- cotangent: bfloat16 [32768, 768], P(('dp', 'fsdp')), may hold values from -6 to 6
Outputs:
- output: bfloat16 [32768, 768], P(('dp', 'fsdp'))
- input_grad: float32 [32768, 768], P(('dp', 'fsdp'))
- grad_query_weight: float32 [768, 768], P('fsdp')
- grad_query_bias: float32 [768], P('fsdp')
- grad_key_weight: float32 [768, 768], P('fsdp')
- grad_value_weight: float32 [768, 768], P('fsdp')
- grad_value_bias: float32 [768], P('fsdp')
- grad_out_weight: float32 [768, 768], P('fsdp')
- grad_out_bias: float32 [768], P('fsdp')
- grad_first_gain: float32 [768], P('fsdp')
- grad_first_shift: float32 [768], P('fsdp')
- grad_expand_weight: float32 [768, 3072], P('fsdp')
- grad_expand_bias: float32 [3072], P('fsdp')
- grad_reduce_weight: float32 [3072, 768], P('fsdp')
- grad_reduce_bias: float32 [768], P('fsdp')
- grad_second_gain: float32 [768], P('fsdp')
- grad_second_shift: float32 [768], P('fsdp')
Inputs may be any that keep to these rules, and one draw needn't show every extreme that they name: `segment_ids`: within a sequence the fragment numbers never fall; every one of the 8 fragments is present, and the longest has exactly 160 tokens.
All inputs are finite; a program needn't handle non-finite values.
Results may differ from a plain program's by a relative error of at most 0.02.
Values may be sent and summed in bfloat16 or wider, within the bound.
A program may use at most 192 MiB of HBM per device.

v0:
```python
import jax
import jax.numpy as jnp
from jax import lax
from jax.sharding import PartitionSpec as P

HEADS = 12
HEAD = 64


def layer_norm(rows, gain, shift):
    average = jnp.mean(rows, axis=-1, keepdims=True)
    centered = rows - average
    rescale = lax.rsqrt(jnp.mean(centered * centered, axis=-1, keepdims=True) + 1e-12)
    normed = centered * rescale
    return (normed * gain.astype(jnp.float32) + shift.astype(jnp.float32), normed, rescale)


def norm_back(gradient, normed, rescale, gain):
    scaled = gradient * gain.astype(jnp.float32)
    inner_mean = jnp.mean(scaled * normed, axis=-1, keepdims=True)
    rows_grad = rescale * (scaled - jnp.mean(scaled, axis=-1, keepdims=True) - normed * inner_mean)
    return (rows_grad, jnp.sum(gradient * normed, axis=0), jnp.sum(gradient, axis=0))


def linear(rows, weight, bias):
    return jnp.dot(rows, weight, preferred_element_type=jnp.float32) + bias.astype(jnp.float32)


def weight_grad(rows, gradient):
    return jnp.einsum("ti,to->io", rows, gradient, preferred_element_type=jnp.float32)


def bias_grad(gradient):
    return jnp.sum(gradient.astype(jnp.float32), axis=0)


def back_rows(gradient, weight):
    return jnp.einsum("to,io->ti", gradient, weight, preferred_element_type=jnp.float32)


def gelu_slope(inner):
    normal_cdf = 0.5 * (1.0 + lax.erf(inner * 0.7071067811865476))
    density = jnp.exp(-0.5 * inner * inner) * 0.3989422804014327
    return normal_cdf + inner * density


def masked_scores(queries, key_rows, fragment):
    scaling = queries.shape[-1] ** (-0.5)
    scores = (
        jnp.einsum("qhd,khd->hqk", queries, key_rows, preferred_element_type=jnp.float32) * scaling
    )
    same_fragment = fragment[:, None] == fragment[None, :]
    return jnp.where(same_fragment[None, :, :], scores, -1000000000.0)


def attend_forward(bundle):
    queries, key_rows, value_rows, fragment = bundle
    scores = masked_scores(queries, key_rows, fragment)
    highest = jnp.max(scores, axis=-1, keepdims=True)
    lifted = jnp.exp(scores - highest)
    totals = jnp.sum(lifted, axis=-1, keepdims=True)
    weights = (lifted / totals).astype(jnp.bfloat16)
    mixed = jnp.einsum("hqk,khd->qhd", weights, value_rows, preferred_element_type=jnp.float32)
    return (mixed.astype(jnp.bfloat16), highest + jnp.log(totals))


def attend_backward(bundle):
    queries, key_rows, value_rows, fragment, mixed_grad, log_totals = bundle
    scaling = queries.shape[-1] ** (-0.5)
    weights = jnp.exp(masked_scores(queries, key_rows, fragment) - log_totals)
    value_grad = jnp.einsum(
        "hqk,qhd->khd", weights.astype(jnp.bfloat16), mixed_grad, preferred_element_type=jnp.float32
    )
    prob_grad = jnp.einsum(
        "qhd,khd->hqk", mixed_grad, value_rows, preferred_element_type=jnp.float32
    )
    score_grad = (
        weights * (prob_grad - jnp.sum(prob_grad * weights, axis=-1, keepdims=True))
    ).astype(jnp.bfloat16)
    query_grad = (
        jnp.einsum("hqk,khd->qhd", score_grad, key_rows, preferred_element_type=jnp.float32)
        * scaling
    )
    key_grad = (
        jnp.einsum("hqk,qhd->khd", score_grad, queries, preferred_element_type=jnp.float32)
        * scaling
    )
    return (
        query_grad.astype(jnp.bfloat16),
        key_grad.astype(jnp.bfloat16),
        value_grad.astype(jnp.bfloat16),
    )


def on_device(
    tokens,
    segment_ids,
    query_weight,
    query_bias,
    key_weight,
    value_weight,
    value_bias,
    out_weight,
    out_bias,
    first_gain,
    first_shift,
    expand_weight,
    expand_bias,
    reduce_weight,
    reduce_bias,
    second_gain,
    second_shift,
    cotangent,
):
    seq_count, seq_length = segment_ids.shape
    shaped = (seq_count, seq_length, HEADS, HEAD)
    attention_set = (
        lax.all_gather(query_weight, "fsdp", axis=0, tiled=True),
        lax.all_gather(query_bias, "fsdp", axis=0, tiled=True),
        lax.all_gather(key_weight, "fsdp", axis=0, tiled=True),
        lax.all_gather(value_weight, "fsdp", axis=0, tiled=True),
        lax.all_gather(value_bias, "fsdp", axis=0, tiled=True),
        lax.all_gather(out_weight, "fsdp", axis=0, tiled=True),
        lax.all_gather(out_bias, "fsdp", axis=0, tiled=True),
        lax.all_gather(first_gain, "fsdp", axis=0, tiled=True),
        lax.all_gather(first_shift, "fsdp", axis=0, tiled=True),
    )
    queries = (
        linear(tokens, attention_set[0], attention_set[1]).astype(jnp.bfloat16).reshape(shaped)
    )
    key_rows = (
        jnp.dot(tokens, attention_set[2], preferred_element_type=jnp.float32)
        .astype(jnp.bfloat16)
        .reshape(shaped)
    )
    value_rows = (
        linear(tokens, attention_set[3], attention_set[4]).astype(jnp.bfloat16).reshape(shaped)
    )
    mixed, log_totals = lax.map(attend_forward, (queries, key_rows, value_rows, segment_ids))
    mixed = mixed.reshape(tokens.shape)
    first_sum = tokens.astype(jnp.float32) + linear(mixed, attention_set[5], attention_set[6])
    hidden, first_normed, first_rescale = layer_norm(first_sum, attention_set[7], attention_set[8])
    hidden_low = hidden.astype(jnp.bfloat16)
    feed_set = (
        lax.all_gather(expand_weight, "fsdp", axis=0, tiled=True),
        lax.all_gather(expand_bias, "fsdp", axis=0, tiled=True),
        lax.all_gather(reduce_weight, "fsdp", axis=0, tiled=True),
        lax.all_gather(reduce_bias, "fsdp", axis=0, tiled=True),
        lax.all_gather(second_gain, "fsdp", axis=0, tiled=True),
        lax.all_gather(second_shift, "fsdp", axis=0, tiled=True),
    )
    inner = linear(hidden_low, feed_set[0], feed_set[1])
    active = jax.nn.gelu(inner, approximate=False).astype(jnp.bfloat16)
    second_sum = hidden + linear(active, feed_set[2], feed_set[3])
    output, second_normed, second_rescale = layer_norm(second_sum, feed_set[4], feed_set[5])
    feed_back = (
        lax.all_gather(expand_weight, "fsdp", axis=0, tiled=True),
        lax.all_gather(expand_bias, "fsdp", axis=0, tiled=True),
        lax.all_gather(reduce_weight, "fsdp", axis=0, tiled=True),
        lax.all_gather(reduce_bias, "fsdp", axis=0, tiled=True),
        lax.all_gather(second_gain, "fsdp", axis=0, tiled=True),
        lax.all_gather(second_shift, "fsdp", axis=0, tiled=True),
    )
    second_grad, grad_second_gain, grad_second_shift = norm_back(
        cotangent.astype(jnp.float32), second_normed, second_rescale, feed_back[4]
    )
    branch_grad = second_grad.astype(jnp.bfloat16)
    grad_reduce = weight_grad(active, branch_grad)
    grad_reduce_bias = bias_grad(branch_grad)
    inner_grad = (back_rows(branch_grad, feed_back[2]) * gelu_slope(inner)).astype(jnp.bfloat16)
    grad_expand = weight_grad(hidden_low, inner_grad)
    grad_expand_bias = bias_grad(inner_grad)
    hidden_grad = second_grad + back_rows(inner_grad, feed_back[0])
    feed_grads = (
        lax.psum_scatter(
            grad_expand.astype(jnp.bfloat16), "fsdp", scatter_dimension=0, tiled=True
        ).astype(jnp.float32),
        lax.psum_scatter(
            grad_expand_bias.astype(jnp.bfloat16), "fsdp", scatter_dimension=0, tiled=True
        ).astype(jnp.float32),
        lax.psum_scatter(
            grad_reduce.astype(jnp.bfloat16), "fsdp", scatter_dimension=0, tiled=True
        ).astype(jnp.float32),
        lax.psum_scatter(
            grad_reduce_bias.astype(jnp.bfloat16), "fsdp", scatter_dimension=0, tiled=True
        ).astype(jnp.float32),
        lax.psum_scatter(
            grad_second_gain.astype(jnp.bfloat16), "fsdp", scatter_dimension=0, tiled=True
        ).astype(jnp.float32),
        lax.psum_scatter(
            grad_second_shift.astype(jnp.bfloat16), "fsdp", scatter_dimension=0, tiled=True
        ).astype(jnp.float32),
    )
    attention_back = (
        lax.all_gather(query_weight, "fsdp", axis=0, tiled=True),
        lax.all_gather(query_bias, "fsdp", axis=0, tiled=True),
        lax.all_gather(key_weight, "fsdp", axis=0, tiled=True),
        lax.all_gather(value_weight, "fsdp", axis=0, tiled=True),
        lax.all_gather(value_bias, "fsdp", axis=0, tiled=True),
        lax.all_gather(out_weight, "fsdp", axis=0, tiled=True),
        lax.all_gather(out_bias, "fsdp", axis=0, tiled=True),
        lax.all_gather(first_gain, "fsdp", axis=0, tiled=True),
        lax.all_gather(first_shift, "fsdp", axis=0, tiled=True),
    )
    first_grad, grad_first_gain, grad_first_shift = norm_back(
        hidden_grad, first_normed, first_rescale, attention_back[7]
    )
    out_grad = first_grad.astype(jnp.bfloat16)
    grad_out = weight_grad(mixed, out_grad)
    grad_out_bias = bias_grad(out_grad)
    mixed_grad = back_rows(out_grad, attention_back[5]).astype(jnp.bfloat16).reshape(shaped)
    query_grad, key_grad, value_grad = lax.map(
        attend_backward, (queries, key_rows, value_rows, segment_ids, mixed_grad, log_totals)
    )
    query_grad = query_grad.reshape(tokens.shape)
    key_grad = key_grad.reshape(tokens.shape)
    value_grad = value_grad.reshape(tokens.shape)
    grad_query = weight_grad(tokens, query_grad)
    grad_query_bias = bias_grad(query_grad)
    grad_key = weight_grad(tokens, key_grad)
    grad_value = weight_grad(tokens, value_grad)
    grad_value_bias = bias_grad(value_grad)
    input_grad = (
        first_grad
        + back_rows(query_grad, attention_back[0])
        + back_rows(key_grad, attention_back[2])
        + back_rows(value_grad, attention_back[3])
    )
    attention_grads = (
        lax.psum_scatter(
            grad_query.astype(jnp.bfloat16), "fsdp", scatter_dimension=0, tiled=True
        ).astype(jnp.float32),
        lax.psum_scatter(
            grad_query_bias.astype(jnp.bfloat16), "fsdp", scatter_dimension=0, tiled=True
        ).astype(jnp.float32),
        lax.psum_scatter(
            grad_key.astype(jnp.bfloat16), "fsdp", scatter_dimension=0, tiled=True
        ).astype(jnp.float32),
        lax.psum_scatter(
            grad_value.astype(jnp.bfloat16), "fsdp", scatter_dimension=0, tiled=True
        ).astype(jnp.float32),
        lax.psum_scatter(
            grad_value_bias.astype(jnp.bfloat16), "fsdp", scatter_dimension=0, tiled=True
        ).astype(jnp.float32),
        lax.psum_scatter(
            grad_out.astype(jnp.bfloat16), "fsdp", scatter_dimension=0, tiled=True
        ).astype(jnp.float32),
        lax.psum_scatter(
            grad_out_bias.astype(jnp.bfloat16), "fsdp", scatter_dimension=0, tiled=True
        ).astype(jnp.float32),
        lax.psum_scatter(
            grad_first_gain.astype(jnp.bfloat16), "fsdp", scatter_dimension=0, tiled=True
        ).astype(jnp.float32),
        lax.psum_scatter(
            grad_first_shift.astype(jnp.bfloat16), "fsdp", scatter_dimension=0, tiled=True
        ).astype(jnp.float32),
    )
    summed = (
        lax.psum(attention_grads[0].astype(jnp.bfloat16), "dp").astype(jnp.float32),
        lax.psum(attention_grads[1].astype(jnp.bfloat16), "dp").astype(jnp.float32),
        lax.psum(attention_grads[2].astype(jnp.bfloat16), "dp").astype(jnp.float32),
        lax.psum(attention_grads[3].astype(jnp.bfloat16), "dp").astype(jnp.float32),
        lax.psum(attention_grads[4].astype(jnp.bfloat16), "dp").astype(jnp.float32),
        lax.psum(attention_grads[5].astype(jnp.bfloat16), "dp").astype(jnp.float32),
        lax.psum(attention_grads[6].astype(jnp.bfloat16), "dp").astype(jnp.float32),
        lax.psum(attention_grads[7].astype(jnp.bfloat16), "dp").astype(jnp.float32),
        lax.psum(attention_grads[8].astype(jnp.bfloat16), "dp").astype(jnp.float32),
        lax.psum(feed_grads[0].astype(jnp.bfloat16), "dp").astype(jnp.float32),
        lax.psum(feed_grads[1].astype(jnp.bfloat16), "dp").astype(jnp.float32),
        lax.psum(feed_grads[2].astype(jnp.bfloat16), "dp").astype(jnp.float32),
        lax.psum(feed_grads[3].astype(jnp.bfloat16), "dp").astype(jnp.float32),
        lax.psum(feed_grads[4].astype(jnp.bfloat16), "dp").astype(jnp.float32),
        lax.psum(feed_grads[5].astype(jnp.bfloat16), "dp").astype(jnp.float32),
    )
    return (
        output.astype(jnp.bfloat16),
        input_grad,
        summed[0],
        summed[1],
        summed[2],
        summed[3],
        summed[4],
        summed[5],
        summed[6],
        summed[7],
        summed[8],
        summed[9],
        summed[10],
        summed[11],
        summed[12],
        summed[13],
        summed[14],
    )


def solution(mesh):
    in_specs = (
        P(("dp", "fsdp"), None),
        P(("dp", "fsdp"), None),
        P("fsdp", None),
        P("fsdp"),
        P("fsdp", None),
        P("fsdp", None),
        P("fsdp"),
        P("fsdp", None),
        P("fsdp"),
        P("fsdp"),
        P("fsdp"),
        P("fsdp", None),
        P("fsdp"),
        P("fsdp", None),
        P("fsdp"),
        P("fsdp"),
        P("fsdp"),
        P(("dp", "fsdp"), None),
    )
    out_specs = (
        P(("dp", "fsdp"), None),
        P(("dp", "fsdp"), None),
        P("fsdp", None),
        P("fsdp"),
        P("fsdp", None),
        P("fsdp", None),
        P("fsdp"),
        P("fsdp", None),
        P("fsdp"),
        P("fsdp"),
        P("fsdp"),
        P("fsdp", None),
        P("fsdp"),
        P("fsdp", None),
        P("fsdp"),
        P("fsdp"),
        P("fsdp"),
    )
    return jax.shard_map(
        on_device, mesh=mesh, in_specs=in_specs, out_specs=out_specs, check_vma=False
    )
```

profile of v0, /device:TPU:0, one launch (start us, length us, event | category | flops | bytes accessed | tf_op | source)
XLA Modules:
  0.0 987.1 jit_solution(2345672940246471056)
XLA Ops:
  19.1 39.4 %all-reduce.18 = (bf16[768]{0:T(1024)(128)(2,1)S(1)}, bf16[768]{0:T(1024)(128)(2,1)S(1)}, bf16[768]{0:T(1024)(128)(2,1)S(1)}, bf16[768]{0:T(1024)(128)(2,1)S(1)}...) all-reduce(bf16[768]{0:T(1024)(128)(2,1)S(1)} %dynamic-update-slice, ...), channel_id=1, replica_groups=mesh['dp'=4,'fsdp'=8] {'fsdp'}, use_global_device_ids=true, to_apply=%add.1 | all-reduce | flops 5376 | bytes 21504
  58.5 2.7 copy.93
  61.2 26.2 %all-gather = bf16[8,1,384]{2,1,0:T(2,128)(2,1)S(1)} all-gather(bf16[1,1,384]{2,1,0:T(2,128)(2,1)S(1)} %reshape.227), channel_id=1, replica_groups=mesh['dp'=4,'fsdp'=8] {'fsdp'}, dimensions={0}, use_global_device_ids=true | all-gather | bytes 6912 | tf_op jit(solution)/shard_map/all_gather | solution.py:146
  90.3 3.8 add_convert_fusion.2
  98.7 2.7 add_convert_fusion.1
  103.7 34.7 %all-gather.12.cloned.1.call-done = bf16[768,768]{1,0:T(8,128)(2,1)} async-done(((bf16[96,768]{1,0:T(8,128)(2,1)}), bf16[768,768]{1,0:T(8,128)(2,1)}) %all-gather.12.cloned.1.call-update) | async-done | bytes 1179664 | tf_op jit(solution)/shard_map/all_gather | solution.py:120
  138.4 4.3 convolution_convert_fusion.3
  144.4 2.4 reshape.197
  149.9 21.0 %while.26 = (s32[]{:T(128)}, bf16[2,512,12,64]{1,3,2,0:T(8,128)(2,1)}, f32[2,12,512,1]{2,1,3,0:T(8,128)S(1)}, bf16[2,512,12,64]{1,3,2,0:T(8,128)(2,1)}, s32[2,51...) while((s32[]{:T(128)}, ...), condition=%wide.region_3.4_spmd, body=%wide.region_0.3_spmd.sunk | while | flops 843704320 | bytes 42172508 | solution.py:139
  150.3 2.1 fusion.149
  152.4 2.6 fusion.150
  155.0 5.5 fusion.151
  160.7 2.1 fusion.149
  162.8 2.6 fusion.150
  165.4 5.5 fusion.151
  170.9 3.0 copy.100
  175.5 4.8 all-gather.14.cloned.1.call-done
  180.3 3.9 fusion.93
  186.2 74.1 %all-gather.16.cloned.1.call-done = bf16[768,3072]{1,0:T(8,128)(2,1)} async-done(((bf16[96,3072]{1,0:T(8,128)(2,1)}), bf16[768,3072]{1,0:T(8,128)(2,1)}) %all-gather.16.cloned.1.call-update) | async-done | bytes 4718608 | tf_op jit(solution)/shard_map/all_gather | solution.py:145
  260.4 50.1 %fusion.59 = (bf16[1024,3072]{1,0:T(8,128)(2,1)}, f32[1024,3072]{1,0:T(8,128)}) fusion(f32[3072]{0:T(1024)S(1)} %bitcast.193, bf16[768,3072]{1,0:T(8,128)(2,1)} %all-gather.16.cloned.1.call-done, f32[1024,768]{0,1:T(8,128)} %copy-done.7, f32[768]{0:T(1024)S(1)} %convert_element_type.228, f32[768]{0:T(1024)S(1)} %convert_element_type.227, ...), kind=kOutput, calls=%fused_computation.68 | convolution fusion | flops 5043388416 | bytes 26765312 | tf_op jit(solution)/shard_map/dot_general | solution.py:26
  310.5 29.6 %all-gather.18.cloned.1.call-done = bf16[3072,768]{1,0:T(8,128)(2,1)} async-done(((bf16[384,768]{1,0:T(8,128)(2,1)}), bf16[3072,768]{1,0:T(8,128)(2,1)}) %all-gather.18.cloned.1.call-update) | async-done | bytes 4718608 | tf_op jit(solution)/shard_map/all_gather | solution.py:147
  340.1 9.4 fusion.94
  350.0 2.1 copy-done.5
  356.0 14.7 %fusion.95 = (bf16[3072]{0:T(1024)(128)(2,1)}, bf16[1024,3072]{1,0:T(8,128)(2,1)}) fusion(f32[1024,3072]{1,0:T(8,128)} %get-tuple-element.302, f32[3072]{0:T(1024)S(1)} %bitcast.194, bf16[1024,768]{0,1:T(8,128)(2,1)S(1)} %get-tuple-element.290, bf16[3072,768]{1,0:T(8,128)(2,1)S(1)} %bitcast.198), kind=kOutput, calls=%fused_computation.144 | convolution fusion | flops 4869583872 | bytes 25184256 | tf_op jit(solution)/shard_map/to,io->ti/dot_general | solution.py:38
  370.7 9.7 multiply_reduce_fusion.1
  383.9 2.6 convolution_convert_fusion.2
  386.5 2.6 copy.104
  389.1 3.9 reshape.199
  392.9 2.9 copy.107
  399.9 48.5 %while.27 = (s32[]{:T(128)}, bf16[2,512,12,64]{1,3,2,0:T(8,128)(2,1)}, bf16[2,512,12,64]{1,3,2,0:T(8,128)(2,1)}, bf16[2,512,12,64]{1,3,2,0:T(8,128)(2,1)}, bf16[...) while((s32[]{:T(128)}, ...), condition=%wide.region_14.15_spmd, body=%wide.region_12.14_spmd.sunk | while | flops 2062673920 | bytes 134941968 | solution.py:212
  402.2 6.9 multiply_reduce_fusion.7
  409.1 7.1 multiply_convert_fusion.4
  416.2 2.0 fusion.162
  418.2 2.0 fusion.161
  420.2 3.9 fusion.163
  426.3 6.9 multiply_reduce_fusion.7
  433.2 7.1 multiply_convert_fusion.4
  442.3 2.1 fusion.161
  444.4 3.9 fusion.163
  448.3 3.1 copy.109
  453.1 2.4 fusion.81
  455.5 2.5 copy.129
  461.5 2.4 fusion.82
  463.9 2.5 copy.131
  469.7 2.4 fusion.83
  472.1 2.5 copy.133
  474.7 4.4 convolution_convert_fusion.4
  479.2 9.8 convolution_convert_fusion.1
  490.4 9.7 convolution_convert_fusion
  505.7 34.7 %all-reduce.17 = (bf16[768]{0:T(1024)(128)(2,1)S(1)}, bf16[768]{0:T(1024)(128)(2,1)S(1)}, bf16[768]{0:T(1024)(128)(2,1)S(1)}, bf16[768]{0:T(1024)(128)(2,1)S(1)}...) all-reduce(bf16[768]{0:T(1024)(128)(2,1)S(1)} %dynamic-update-slice, ...), channel_id=1, replica_groups=mesh['dp'=4,'fsdp'=8] {'fsdp'}, use_global_device_ids=true, to_apply=%add.7 | all-reduce | flops 9984 | bytes 39936
  541.0 5.7 all-reduce.19
  551.4 4.5 fusion.96
  556.0 3.1 fusion.97
  560.8 27.7 %reduce-scatter.21.cloned.1.call-done = bf16[96,768]{1,0:T(8,128)(2,1)} async-done(((bf16[768,768]{1,0:T(8,128)(2,1)}), bf16[96,768]{1,0:T(8,128)(2,1)}) %reduce-scatter.21.cloned.1.call-update) | async-done | bytes 147472
  590.2 65.5 %reduce-scatter.23.cloned.1.call-done = bf16[96,768]{1,0:T(8,128)(2,1)} async-done(((bf16[768,768]{1,0:T(8,128)(2,1)}), bf16[96,768]{1,0:T(8,128)(2,1)}) %reduce-scatter.23.cloned.1.call-update) | async-done | bytes 147472
  657.5 65.9 %reduce-scatter.13.cloned.1.call-done = bf16[96,768]{1,0:T(8,128)(2,1)} async-done(((bf16[768,768]{1,0:T(8,128)(2,1)}), bf16[96,768]{1,0:T(8,128)(2,1)}) %reduce-scatter.13.cloned.1.call-update) | async-done | bytes 147472 | tf_op jit(solution)/shard_map/reduce_scatter | solution.py:245
  723.4 98.4 %reduce-scatter.15.cloned.1.call-done = bf16[96,3072]{1,0:T(8,128)(2,1)} async-done(((bf16[768,3072]{1,0:T(8,128)(2,1)}), bf16[96,3072]{1,0:T(8,128)(2,1)}) %reduce-scatter.15.cloned.1.call-update) | async-done | bytes 589840 | tf_op jit(solution)/shard_map/reduce_scatter | solution.py:175
  821.8 98.9 %reduce-scatter.17.cloned.1.call-done = bf16[384,768]{1,0:T(8,128)(2,1)} async-done(((bf16[3072,768]{1,0:T(8,128)(2,1)}), bf16[384,768]{1,0:T(8,128)(2,1)}) %reduce-scatter.17.cloned.1.call-update) | async-done | bytes 589840 | tf_op jit(solution)/shard_map/reduce_scatter | solution.py:181
  920.7 6.8 add_add_fusion
  927.6 3.9 copy.116
  933.2 2.6 copy.115
  935.8 36.6 %all-reduce.23.cloned.1.call-done = (bf16[96,768]{0,1:T(8,128)(2,1)}, bf16[96,768]{0,1:T(8,128)(2,1)}, bf16[96,768]{0,1:T(8,128)(2,1)}, bf16[96,768]{1,0:T(8,128...) async-done(((bf16[96,768]{0,1:T(8,128)(2,1)}, bf16[96,768]{0,1:T(8,128)(2,1)}, bf16[96,768]{0,1:T(8,128)(2,1)}, bf16[96,768]{1,0:T(8,128)(2,1)}, ...) | async-done | bytes 1769488 | tf_op jit(solution)/shard_map/psum | solution.py:259
  972.4 2.2 convert_element_type.260
  974.7 2.2 convert_element_type.263
  (267 shorter events, 77.0 us)
Async XLA Ops:
  7.2 54.0 %copy-start.53 = (bf16[384]{0:T(512)(128)(2,1)S(1)}, bf16[384]{0:T(512)(128)(2,1)}, u32[]{:S(2)}) copy-start(bf16[384]{0:T(512)(128)(2,1)} %param.34) | copy-start | bytes 2308
  7.2 81.5 %copy-start.11 = (bf16[1024,768]{1,0:T(8,128)(2,1)S(1)}, bf16[1024,768]{1,0:T(8,128)(2,1)}, u32[]{:S(2)}) copy-start(bf16[1024,768]{1,0:T(8,128)(2,1)} %param.39) | copy-start | bytes 4718596
  7.2 83.1 %all-gather.8.cloned.1.call-start = ((), (), s32[]{:S(2)}) async-start(), calls=%async_computation.6 | async-start | bytes 1327104 | tf_op jit(solution)/shard_map/all_gather | solution.py:121
  7.9 90.6 %all-gather.10.cloned.1.call-start = ((), (), s32[]{:S(2)}) async-start(), calls=%async_computation.7 | async-start | bytes 1327104 | tf_op jit(solution)/shard_map/all_gather | solution.py:118
  8.7 129.7 %all-gather.12.cloned.1.call-start = ((), (), s32[]{:S(2)}) async-start(), calls=%async_computation.8 | async-start | bytes 1327104 | tf_op jit(solution)/shard_map/all_gather | solution.py:120
  9.4 170.9 %all-gather.14.cloned.1.call-start = ((), (), s32[]{:S(2)}) async-start(), calls=%async_computation.9 | async-start | bytes 1327104 | tf_op jit(solution)/shard_map/all_gather | solution.py:123
  10.0 250.4 %all-gather.16.cloned.1.call-start = ((), (), s32[]{:S(2)}) async-start(), calls=%async_computation.10 | async-start | bytes 5308416 | tf_op jit(solution)/shard_map/all_gather | solution.py:145
  10.6 329.5 %all-gather.18.cloned.1.call-start = ((), (), s32[]{:S(2)}) async-start(), calls=%async_computation.11 | async-start | bytes 5308416 | tf_op jit(solution)/shard_map/all_gather | solution.py:147
  11.2 547.9 %reduce-scatter.19.cloned.1.call-start = ((), (), s32[]{:S(2)}) async-start(), calls=%async_computation.15 | async-start | bytes 1327104
  58.5 31.8 %copy-start.17 = (bf16[1024,768]{1,0:T(8,128)(2,1)S(1)}, bf16[1024,768]{1,0:T(8,128)(2,1)}, u32[]{:S(2)}) copy-start(bf16[1024,768]{1,0:T(8,128)(2,1)} %param.22) | copy-start | bytes 4718596
  61.2 319.2 %copy-start.40 = (f32[768]{0:T(1024)}, f32[768]{0:T(1024)S(1)}, u32[]{:S(2)}) copy-start(f32[768]{0:T(1024)S(1)} %convert_element_type.227) | copy-start | bytes 9220
  61.2 278.9 %copy-start.48 = (f32[768]{0:T(1024)}, f32[768]{0:T(1024)S(1)}, u32[]{:S(2)}) copy-start(f32[768]{0:T(1024)S(1)} %convert_element_type.228) | copy-start | bytes 9220
  146.8 3.1 copy-start.33
  184.2 196.2 %copy-start.38 = (f32[1024]{0:T(1024)}, f32[1024]{0:T(1024)S(1)}, u32[]{:S(2)}) copy-start(f32[1024]{0:T(1024)S(1)} %broadcast_multiply_fusion.5) | copy-start | bytes 12292
  186.2 194.2 %copy-start.42 = (f32[1024]{0:T(1024)}, f32[1024]{0:T(1024)S(1)}, u32[]{:S(2)}) copy-start(f32[1024]{0:T(1024)S(1)} %add_rsqrt_fusion.1) | copy-start | bytes 12292
  260.4 79.8 %copy-start.50 = (f32[768]{0:T(1024)S(1)}, f32[768]{0:T(1024)}, u32[]{:S(2)}) copy-start(f32[768]{0:T(1024)} %convert_element_type.232) | copy-start | bytes 9220
  349.6 21.1 %copy-start = (f32[1024,768]{0,1:T(8,128)}, f32[1024,768]{0,1:T(8,128)S(1)}, u32[]{:S(2)}) copy-start(f32[1024,768]{0,1:T(8,128)S(1)} %get-tuple-element.304) | copy-start | bytes 9437188
  349.6 2.5 copy-start.5
  349.6 2.5 copy-start.34
  349.6 21.0 %copy-start.31 = (f32[1024]{0:T(1024)}, f32[1024]{0:T(1024)S(1)}, u32[]{:S(2)}) copy-start(f32[1024]{0:T(1024)S(1)} %broadcast_multiply_fusion.4) | copy-start | bytes 12292
  349.6 6.3 slice-start.2
  352.1 18.5 %copy-start.36 = (f32[1024]{0:T(1024)}, f32[1024]{0:T(1024)S(1)}, u32[]{:S(2)}) copy-start(f32[1024]{0:T(1024)S(1)} %add_rsqrt_fusion) | copy-start | bytes 12292
  352.1 3.8 slice-start.3
  354.1 16.6 %slice-start = ((s8[4718592]{0:T(1024)(128)(4,1)}), s8[4194304]{0:T(1024)(128)(4,1)S(1)}, s32[]{:S(2)}) async-start(s8[4718592]{0:T(1024)(128)(4,1)} %bitcast.195), calls=%async_computation.19 | async-start | bytes 8388608
  355.9 14.7 %copy-start.25 = (bf16[1024,768]{0,1:T(8,128)(2,1)}, bf16[1024,768]{0,1:T(8,128)(2,1)S(1)}, u32[]{:S(2)}) copy-start(bf16[1024,768]{0,1:T(8,128)(2,1)S(1)} %get-tuple-element.290) | copy-start | bytes 4718596
  356.0 14.7 %copy-start.8 = (f32[1024,768]{0,1:T(8,128)S(1)}, f32[1024,768]{0,1:T(8,128)}, u32[]{:S(2)}) copy-start(f32[1024,768]{0,1:T(8,128)} %copy-done.7) | copy-start | bytes 9437188
  356.0 14.7 %slice-start.1 = ((s8[4718592]{0:T(1024)(128)(4,1)}), s8[524288]{0:T(1024)(128)(4,1)S(1)}, s32[]{:S(2)}) async-start(s8[4718592]{0:T(1024)(128)(4,1)} %bitcast.195), calls=%async_computation.20 | async-start | bytes 1048576
  380.4 3.5 copy-start.55
  400.0 2.1 copy-start.2
  409.1 7.1 copy-start.14
  433.2 7.1 copy-start.14
  448.3 4.7 copy-start.19
  455.5 2.8 copy-start.16
  458.0 130.5 %reduce-scatter.21.cloned.1.call-start = ((), (), s32[]{:S(2)}) async-start(), calls=%async_computation.16 | async-start | bytes 1327104
  463.9 2.6 copy-start.6
  466.4 189.4 %reduce-scatter.23.cloned.1.call-start = ((), (), s32[]{:S(2)}) async-start(), calls=%async_computation.17 | async-start | bytes 1327104
  472.0 2.6 copy-start.20
  474.6 4.5 copy-start.39
  474.6 4.5 copy-start.41
  474.6 4.5 copy-start.43
  474.6 4.5 copy-start.49
  474.6 248.8 %reduce-scatter.13.cloned.1.call-start = ((), (), s32[]{:S(2)}) async-start(), calls=%async_computation.12 | async-start | bytes 1327104 | tf_op jit(solution)/shard_map/reduce_scatter | solution.py:245
  479.1 342.7 %reduce-scatter.15.cloned.1.call-start = ((), (), s32[]{:S(2)}) async-start(), calls=%async_computation.13 | async-start | bytes 5308416 | tf_op jit(solution)/shard_map/reduce_scatter | solution.py:175
  489.0 431.7 %reduce-scatter.17.cloned.1.call-start = ((), (), s32[]{:S(2)}) async-start(), calls=%async_computation.14 | async-start | bytes 5308416 | tf_op jit(solution)/shard_map/reduce_scatter | solution.py:181
  500.1 3.1 copy-start.56
  500.1 5.5 copy-start.44
  500.1 5.5 copy-start.45
  500.1 5.5 copy-start.46
  500.2 5.5 copy-start.47
  500.2 5.5 copy-start.51
  500.2 5.5 copy-start.52
  500.2 472.2 %all-reduce.23.cloned.1.call-start = ((), (), s32[]{:S(2)}) async-start(), calls=%async_computation.18 | async-start | bytes 3833856 | tf_op jit(solution)/shard_map/psum | solution.py:259
  501.8 49.6 %copy-start.22 = (bf16[96,8,2,512]{3,1,2,0:T(8,128)(2,1)S(1)}, bf16[96,8,2,512]{3,1,2,0:T(8,128)(2,1)}, u32[]{:S(2)}) copy-start(bf16[96,8,2,512]{3,1,2,0:T(8,128)(2,1)} %copy-done.21) | copy-start | bytes 4718596
  551.4 4.6 copy-start.24
  551.4 4.6 copy-start.54
  556.0 364.7 %copy-start.10 = (f32[1024,768]{0,1:T(8,128)S(1)}, f32[1024,768]{0,1:T(8,128)}, u32[]{:S(2)}) copy-start(f32[1024,768]{0,1:T(8,128)} %copy-done.9) | copy-start | bytes 9437188
  927.5 4.0 copy-start.1
  927.5 4.0 copy-start.32
  927.5 4.0 copy-start.35
  927.5 4.0 copy-start.37
  972.4 4.4 copy-start.30
  972.4 5.1 copy-start.29
  972.4 6.0 copy-start.28
  972.4 6.9 copy-start.27
  (15 other events, 26.0 us)
Sparse Core Ops, SparseCore 0:
  10.2 44.1 all-gather.7
  56.5 39.7 all-gather.9
  98.6 39.7 all-gather.11
  140.4 39.7 all-gather.13
  182.3 78.0 all-gather.15
  262.4 77.6 all-gather.17
  458.1 63.1 reduce-scatter.18
  524.7 63.7 reduce-scatter.20
  591.9 63.8 reduce-scatter.22
  659.6 63.8 reduce-scatter.12
  727.1 94.6 reduce-scatter.14
  825.3 95.3 reduce-scatter.16
  924.1 48.3 all-reduce.22
where the time goes:
time: 995 us; the launch traced here: 987 us
  waiting for transfers between devices  540 us (54%)
  matrix products  195 us (20%)
  blocking collectives  106 us (11%)
  local copies, waits for them, and re-layouts  85.5 us (9%)
  other arithmetic  41.6 us (4%)
  between operations  17.1 us (2%)
    reduce_scatter x1, waiting for transfers between devices, on_device(): lax.psum_scatter(grad_reduce.astype(jnp.bfloat16), 'fsdp', scatter_dimens...  98.9 us
    reduce_scatter x1, waiting for transfers between devices, on_device(): lax.psum_scatter(grad_expand.astype(jnp.bfloat16), 'fsdp', scatter_dimens...  98.4 us
    unnamed x16, waiting for transfers between devices  97 us
    all_gather x1, waiting for transfers between devices, on_device(): lax.all_gather(expand_weight, 'fsdp', axis=0, tiled=True)  74.1 us
    unnamed x2, blocking collectives  74 us
    dot_general x5, matrix products, linear(): jnp.dot(rows, weight, preferred_element_type=jnp.float32)  69.9 us
    reduce_scatter x1, waiting for transfers between devices, on_device(): lax.psum_scatter(grad_out.astype(jnp.bfloat16), 'fsdp', scatter_dimension...  65.9 us
    unnamed x156, local copies, waits for them, and re-layouts  48.6 us
  transfers between devices with their start and end apart: 13, of which 10 were waited for; matrix products, arithmetic and copies ran while one was open for 19% of the time, Pallas kernels for 0%

commit v1 on v0

--- a/solution.py
+++ b/solution.py
@@ -5,6 +5,36 @@
 
 HEADS = 12
 HEAD = 64
+
+
+def body_serve(row_data, dim_no):
+    row_data = jnp.moveaxis(row_data, 0, dim_no)
+    arr_now = row_data.shape
+    item_now = row_data.reshape(
+        *arr_now[:dim_no], arr_now[dim_no] * arr_now[dim_no + 1], *arr_now[dim_no + 2 :]
+    )
+    return item_now
+
+
+def wait_spans_all(z_in, mesh_ax, dim_i):
+    workers = lax.axis_size(mesh_ax)
+    pieces_in = [(hop_no, (hop_no + 1) % workers) for hop_no in range(workers)]
+    kept_rows = [(dd, pp) for pp, dd in pieces_in]
+    f_now, finding = ([], [])
+    for dev_i in range(workers - 1):
+        if dev_i % 2 == 0:
+            found_now = lax.ppermute(f_now[-1] if f_now else z_in, mesh_ax, pieces_in)
+            f_now.append(found_now)
+        else:
+            r2 = lax.ppermute(finding[-1] if finding else z_in, mesh_ax, kept_rows)
+            finding.append(r2)
+    seen_now = jnp.stack([*f_now[::-1], z_in, *finding], 0)
+    side_arr = lax.axis_index(mesh_ax)
+    t_next = len(f_now)
+    part_next = side_arr - t_next
+    seen_now = seen_now[(jnp.arange(workers) - part_next) % workers]
+    val2 = body_serve(seen_now, dim_i)
+    return val2
 
 
 def layer_norm(rows, gain, shift):
@@ -117,7 +147,7 @@
     attention_set = (
         lax.all_gather(query_weight, "fsdp", axis=0, tiled=True),
         lax.all_gather(query_bias, "fsdp", axis=0, tiled=True),
-        lax.all_gather(key_weight, "fsdp", axis=0, tiled=True),
+        wait_spans_all(key_weight, "fsdp", 0),
         lax.all_gather(value_weight, "fsdp", axis=0, tiled=True),
         lax.all_gather(value_bias, "fsdp", axis=0, tiled=True),
         lax.all_gather(out_weight, "fsdp", axis=0, tiled=True),

time: 995 us -> 956 us (0.961)
  waiting for transfers between devices: 540 us -> 485 us
  starting transfers between devices: 0.98 us -> 13.6 us
    all_gather x1, waiting for transfers between devices: 34.7 us -> 0.01 us  [on_device(): lax.all_gather(key_weight, 'fsdp', axis=0, tiled=True)]
    all_gather x1, waiting for transfers between devices: 74.1 us -> 41.2 us  [on_device(): lax.all_gather(expand_weight, 'fsdp', axis=0, tiled=True)]
    ppermute x0 -> x7, waiting for transfers between devices: none -> 18.6 us  [the longest x4 16.3 us: wait_spans_all(): found_now = lax.ppermute(f_now[-1] if f_now else z_in, mesh_ax, pieces_in)]
    ppermute x0 -> x7, starting transfers between devices: none -> 12.6 us  [the longest x3 9.55 us: wait_spans_all(): r2 = lax.ppermute(finding[-1] if finding else z_in, mesh_ax, kept_rows)]
    unnamed x156 -> x161, local copies, waits for them, and re-layouts: 48.6 us -> 50.6 us
  transfers between devices with their start and end apart: 13 -> 20, of which waited for: 10 -> 12; matrix products, arithmetic and copies ran while one was open for 19% -> 33% of each run, Pallas kernels for 0% -> 0%
where the time goes in v1:
time: 956 us; the launch traced here: 950 us
  waiting for transfers between devices  485 us (51%)
  matrix products  196 us (21%)
  blocking collectives  104 us (11%)
  local copies, waits for them, and re-layouts  91.3 us (10%)
  other arithmetic  41.6 us (4%)
  between operations  17.2 us (2%)
  starting transfers between devices  13.6 us (1%)
    reduce_scatter x1, waiting for transfers between devices, on_device(): lax.psum_scatter(grad_expand.astype(jnp.bfloat16), 'fsdp', scatter_dimens...  98.9 us
    reduce_scatter x1, waiting for transfers between devices, on_device(): lax.psum_scatter(grad_reduce.astype(jnp.bfloat16), 'fsdp', scatter_dimens...  98.4 us
    unnamed x16, waiting for transfers between devices  95.7 us
    unnamed x2, blocking collectives  72.3 us
    dot_general x5, matrix products, linear(): jnp.dot(rows, weight, preferred_element_type=jnp.float32)  71.5 us
    reduce_scatter x1, waiting for transfers between devices, on_device(): lax.psum_scatter(grad_out.astype(jnp.bfloat16), 'fsdp', scatter_dimension...  65.9 us
    unnamed x161, local copies, waits for them, and re-layouts  50.6 us
    dot_general x6, matrix products, back_rows(): jnp.einsum('to,io->ti', gradient, weight, preferred_element_type=jnp.floa...  43.2 us
  transfers between devices with their start and end apart: 20, of which 12 were waited for; matrix products, arithmetic and copies ran while one was open for 33% of the time, Pallas kernels for 0%

profile of v1, /device:TPU:0, one launch (start us, length us, event | category | flops | bytes accessed | tf_op | source)
XLA Modules:
  0.0 949.8 jit_solution(11030017601277436776)
XLA Ops:
  10.6 3.0 collective-permute-start
  13.7 7.1 collective-permute-done
  20.8 4.7 collective-permute-start.4
  25.5 6.2 collective-permute-done.1
  31.8 4.8 collective-permute-start.5
  36.6 3.0 collective-permute-done.2
  47.4 37.6 %all-reduce.18 = (bf16[768]{0:T(1024)(128)(2,1)S(1)}, bf16[768]{0:T(1024)(128)(2,1)S(1)}, bf16[768]{0:T(1024)(128)(2,1)S(1)}, bf16[768]{0:T(1024)(128)(2,1)S(1)}...) all-reduce(bf16[768]{0:T(1024)(128)(2,1)S(1)} %dynamic-update-slice, ...), channel_id=1, replica_groups=mesh['dp'=4,'fsdp'=8] {'fsdp'}, use_global_device_ids=true, to_apply=%add.1 | all-reduce | flops 5376 | bytes 21504
  85.0 2.6 copy.92
  87.7 26.1 %all-gather = bf16[8,1,384]{2,1,0:T(2,128)(2,1)S(1)} all-gather(bf16[1,1,384]{2,1,0:T(2,128)(2,1)S(1)} %reshape.288), channel_id=1, replica_groups=mesh['dp'=4,'fsdp'=8] {'fsdp'}, dimensions={0}, use_global_device_ids=true | all-gather | bytes 6912 | tf_op jit(solution)/shard_map/all_gather | solution.py:176
  119.7 2.4 collective-permute-done.6
  123.7 2.7 fusion.81
  128.3 4.3 add_convert_fusion.2
  134.3 2.4 reshape.247
  136.6 3.1 copy.95
  139.7 3.8 add_convert_fusion.1
  145.2 2.4 reshape.248
  150.7 20.7 %while.26 = (s32[]{:T(128)}, bf16[2,512,12,64]{1,3,2,0:T(8,128)(2,1)}, f32[2,12,512,1]{2,1,3,0:T(8,128)S(1)}, bf16[2,512,12,64]{1,3,2,0:T(8,128)(2,1)}, s32[2,51...) while((s32[]{:T(128)}, ...), condition=%wide.region_3.4_spmd, body=%wide.region_0.3_spmd.sunk | while | flops 843704320 | bytes 42172508 | solution.py:169
  153.0 2.6 fusion.153
  155.6 5.5 fusion.154
  163.3 2.6 fusion.153
  165.9 5.5 fusion.154
  171.4 3.0 copy.98
  176.0 3.9 fusion.96
  182.0 41.2 %all-gather.14.cloned.1.call-done = bf16[768,3072]{1,0:T(8,128)(2,1)} async-done(((bf16[96,3072]{1,0:T(8,128)(2,1)}), bf16[768,3072]{1,0:T(8,128)(2,1)}) %all-gather.14.cloned.1.call-update) | async-done | bytes 4718608 | tf_op jit(solution)/shard_map/all_gather | solution.py:175
  223.2 50.0 %fusion.59 = (bf16[1024,3072]{1,0:T(8,128)(2,1)}, f32[1024,3072]{1,0:T(8,128)}) fusion(f32[3072]{0:T(1024)S(1)} %bitcast.215, bf16[768,3072]{1,0:T(8,128)(2,1)} %all-gather.14.cloned.1.call-done, f32[1024,768]{0,1:T(8,128)} %copy-done.7, f32[768]{0:T(1024)S(1)} %convert_element_type.232, f32[768]{0:T(1024)S(1)} %convert_element_type.231, ...), kind=kOutput, calls=%fused_computation.69 | convolution fusion | flops 5043388416 | bytes 26765312 | tf_op jit(solution)/shard_map/dot_general | solution.py:56
  273.2 29.7 %all-gather.16.cloned.1.call-done = bf16[3072,768]{1,0:T(8,128)(2,1)} async-done(((bf16[384,768]{1,0:T(8,128)(2,1)}), bf16[3072,768]{1,0:T(8,128)(2,1)}) %all-gather.16.cloned.1.call-update) | async-done | bytes 4718608 | tf_op jit(solution)/shard_map/all_gather | solution.py:177
  302.9 9.4 fusion.97
  318.8 14.7 %fusion.98 = (bf16[3072]{0:T(1024)(128)(2,1)}, bf16[1024,3072]{1,0:T(8,128)(2,1)}) fusion(f32[1024,3072]{1,0:T(8,128)} %get-tuple-element.302, f32[3072]{0:T(1024)S(1)} %bitcast.216, bf16[1024,768]{0,1:T(8,128)(2,1)S(1)} %get-tuple-element.290, bf16[3072,768]{1,0:T(8,128)(2,1)S(1)} %bitcast.220), kind=kOutput, calls=%fused_computation.161 | convolution fusion | flops 4869583872 | bytes 25184256 | tf_op jit(solution)/shard_map/to,io->ti/dot_general | solution.py:68
  333.5 9.7 %multiply_reduce_fusion.1 = (bf16[768]{0:T(1024)(128)(2,1)}, f32[1024]{0:T(1024)S(1)}, f32[1024]{0:T(1024)S(1)}, bf16[768]{0:T(1024)(128)(2,1)}, f32[1024,768]{0,1:T(8,128)S(1)}) fusion(f32[1024,768]{0,1:T(8,128)S(1)} %copy-done.8, f32[1024]{0:T(1024)S(1)} %add_rsqrt_fusion.1, f32[1024]{0:T(1024)S(1)} %broadcast_multiply_fusion.5, ...), kind=kOutput, calls=%fused_computation.102 | convolution fusion | flops 4845989888 | bytes 22062080 | tf_op jit(solution)/shard_map/to,io->ti/dot_general | solution.py:68
  346.7 2.7 convolution_convert_fusion.2
  349.3 2.6 copy.102
  351.9 3.9 reshape.252
  355.8 2.9 copy.105
  362.7 48.4 %while.27 = (s32[]{:T(128)}, bf16[2,512,12,64]{1,3,2,0:T(8,128)(2,1)}, bf16[2,512,12,64]{1,3,2,0:T(8,128)(2,1)}, bf16[2,512,12,64]{1,3,2,0:T(8,128)(2,1)}, bf16[...) while((s32[]{:T(128)}, ...), condition=%wide.region_14.15_spmd, body=%wide.region_12.14_spmd.sunk | while | flops 2062673920 | bytes 134941968 | solution.py:242
  365.0 6.9 multiply_reduce_fusion.7
  371.9 7.1 multiply_convert_fusion.4
  383.1 3.9 fusion.166
  389.1 6.9 multiply_reduce_fusion.7
  396.0 7.1 multiply_convert_fusion.4
  407.2 3.9 fusion.166
  411.1 3.1 copy.107
  415.9 2.4 fusion.82
  418.3 2.5 copy.127
  424.2 2.4 fusion.83
  426.6 2.5 copy.129
  432.4 2.4 fusion.84
  434.8 2.5 copy.131
  437.4 4.4 convolution_convert_fusion.4
  441.9 9.1 convolution_convert_fusion
  451.7 9.8 %convolution_convert_fusion.1 = bf16[768,3072]{1,0:T(8,128)(2,1)} fusion(bf16[1024,3072]{1,0:T(8,128)(2,1)} %get-tuple-element.307, f32[1024,768]{0,1:T(8,128)} %copy-done.7, f32[768]{0:T(1024)S(1)} %copy-done.49, f32[768]{0:T(1024)S(1)} %copy-done.41, f32[1024]{0:T(1024)S(1)} %copy-done.43, f32[1024]{0:T(1024)S(1)} %copy-done.39), kind=kOutput, calls=%fused_computation.92 | convolution fusion | flops 4838129664 | bytes 14170112 | tf_op jit(solution)/shard_map/ti,to->io/dot_general | solution.py:60
  467.0 34.7 %all-reduce.17 = (bf16[768]{0:T(1024)(128)(2,1)S(1)}, bf16[768]{0:T(1024)(128)(2,1)S(1)}, bf16[768]{0:T(1024)(128)(2,1)S(1)}, bf16[768]{0:T(1024)(128)(2,1)S(1)}...) all-reduce(bf16[768]{0:T(1024)(128)(2,1)S(1)} %dynamic-update-slice, ...), channel_id=1, replica_groups=mesh['dp'=4,'fsdp'=8] {'fsdp'}, use_global_device_ids=true, to_apply=%add.7 | all-reduce | flops 9984 | bytes 39936
  502.4 6.1 all-reduce.19
  513.2 4.4 fusion.99
  517.7 5.0 fusion.100
  524.4 27.0 %reduce-scatter.21.cloned.1.call-done = bf16[96,768]{1,0:T(8,128)(2,1)} async-done(((bf16[768,768]{1,0:T(8,128)(2,1)}), bf16[96,768]{1,0:T(8,128)(2,1)}) %reduce-scatter.21.cloned.1.call-update) | async-done | bytes 147472
  553.1 65.5 %reduce-scatter.23.cloned.1.call-done = bf16[96,768]{1,0:T(8,128)(2,1)} async-done(((bf16[768,768]{1,0:T(8,128)(2,1)}), bf16[96,768]{1,0:T(8,128)(2,1)}) %reduce-scatter.23.cloned.1.call-update) | async-done | bytes 147472
  620.3 65.9 %reduce-scatter.13.cloned.1.call-done = bf16[96,768]{1,0:T(8,128)(2,1)} async-done(((bf16[768,768]{1,0:T(8,128)(2,1)}), bf16[96,768]{1,0:T(8,128)(2,1)}) %reduce-scatter.13.cloned.1.call-update) | async-done | bytes 147472 | tf_op jit(solution)/shard_map/reduce_scatter | solution.py:275
  686.2 98.4 %reduce-scatter.17.cloned.1.call-done = bf16[384,768]{1,0:T(8,128)(2,1)} async-done(((bf16[3072,768]{1,0:T(8,128)(2,1)}), bf16[384,768]{1,0:T(8,128)(2,1)}) %reduce-scatter.17.cloned.1.call-update) | async-done | bytes 589840 | tf_op jit(solution)/shard_map/reduce_scatter | solution.py:211
  784.5 98.9 %reduce-scatter.15.cloned.1.call-done = bf16[96,3072]{1,0:T(8,128)(2,1)} async-done(((bf16[768,3072]{1,0:T(8,128)(2,1)}), bf16[96,3072]{1,0:T(8,128)(2,1)}) %reduce-scatter.15.cloned.1.call-update) | async-done | bytes 589840 | tf_op jit(solution)/shard_map/reduce_scatter | solution.py:205
  883.4 6.8 add_add_fusion
  890.3 3.9 copy.114
  895.9 2.6 copy.113
  898.5 36.6 %all-reduce.23.cloned.1.call-done = (bf16[96,768]{0,1:T(8,128)(2,1)}, bf16[96,768]{0,1:T(8,128)(2,1)}, bf16[96,768]{0,1:T(8,128)(2,1)}, bf16[96,768]{1,0:T(8,128...) async-done(((bf16[96,768]{0,1:T(8,128)(2,1)}, bf16[96,768]{0,1:T(8,128)(2,1)}, bf16[96,768]{0,1:T(8,128)(2,1)}, bf16[96,768]{1,0:T(8,128)(2,1)}, ...) | async-done | bytes 1769488 | tf_op jit(solution)/shard_map/psum | solution.py:289
  935.1 2.2 convert_element_type.264
  (289 shorter events, 91.6 us)
Async XLA Ops:
  7.2 80.5 %copy-start.53 = (bf16[384]{0:T(512)(128)(2,1)S(1)}, bf16[384]{0:T(512)(128)(2,1)}, u32[]{:S(2)}) copy-start(bf16[384]{0:T(512)(128)(2,1)} %param.34) | copy-start | bytes 2308
  7.2 107.8 %copy-start.11 = (bf16[1024,768]{1,0:T(8,128)(2,1)S(1)}, bf16[1024,768]{1,0:T(8,128)(2,1)}, u32[]{:S(2)}) copy-start(bf16[1024,768]{1,0:T(8,128)(2,1)} %param.39) | copy-start | bytes 4718596
  7.2 121.0 %all-gather.8.cloned.1.call-start = ((), (), s32[]{:S(2)}) async-start(), calls=%async_computation.6 | async-start | bytes 1327104 | tf_op jit(solution)/shard_map/all_gather | solution.py:151
  7.9 131.8 %all-gather.10.cloned.1.call-start = ((), (), s32[]{:S(2)}) async-start(), calls=%async_computation.7 | async-start | bytes 1327104 | tf_op jit(solution)/shard_map/all_gather | solution.py:148
  8.7 167.3 %all-gather.12.cloned.1.call-start = ((), (), s32[]{:S(2)}) async-start(), calls=%async_computation.8 | async-start | bytes 1327104 | tf_op jit(solution)/shard_map/all_gather | solution.py:153
  9.4 213.7 %all-gather.14.cloned.1.call-start = ((), (), s32[]{:S(2)}) async-start(), calls=%async_computation.9 | async-start | bytes 5308416 | tf_op jit(solution)/shard_map/all_gather | solution.py:175
  10.0 292.9 %all-gather.16.cloned.1.call-start = ((), (), s32[]{:S(2)}) async-start(), calls=%async_computation.10 | async-start | bytes 5308416 | tf_op jit(solution)/shard_map/all_gather | solution.py:177
  10.6 507.1 %all-gather.18.cloned.1.call-start = ((), (), s32[]{:S(2)}) async-start(), calls=%async_computation.11 | async-start | bytes 1327104 | tf_op jit(solution)/shard_map/all_gather | solution.py:227
  10.6 10.1 %collective-permute-start = (bf16[96,768]{1,0:T(8,128)(2,1)}, bf16[96,768]{1,0:T(8,128)(2,1)S(1)}, u32[]{:S(2)}, u32[]{:S(2)}) collective-permute-start(bf16[96,768]{1,0:T(8,128)(2,1)} %param.26), channel_id=1, source_target_pairs={{0,1},{1,2},{2,3},{3,4},{4,5},{5,6},{6,7},{7,0},{8,9},{9,10},{10,1... | collective-permute-start | bytes 442376 | tf_op jit(solution)/shard_map/ppermute | solution.py:26
  20.8 10.9 %collective-permute-start.1 = (bf16[96,768]{1,0:T(8,128)(2,1)S(1)}, bf16[96,768]{1,0:T(8,128)(2,1)S(1)}, u32[]{:S(2)}, u32[]{:S(2)}) collective-permute-start(bf16[96,768]{1,0:T(8,128)(2,1)S(1)} %collective-permute-done), channel_id=1, source_target_pairs={{0,1},{1,2},{2,3},{3,4},{4,5},{5,6},{6,7},{7,0},{8,9},{9,10},{10,1... | collective-permute-start | bytes 442376 | tf_op jit(solution)/shard_map/ppermute | solution.py:26
  20.8 11.0 %collective-permute-start.4 = (bf16[96,768]{1,0:T(8,128)(2,1)}, bf16[96,768]{1,0:T(8,128)(2,1)S(1)}, u32[]{:S(2)}, u32[]{:S(2)}) collective-permute-start(bf16[96,768]{1,0:T(8,128)(2,1)} %param.26), channel_id=1, source_target_pairs={{1,0},{2,1},{3,2},{4,3},{5,4},{6,5},{7,6},{0,7},{9,8},{10,9},{11,1... | collective-permute-start | bytes 442376 | tf_op jit(solution)/shard_map/ppermute | solution.py:29
  31.7 7.8 collective-permute-start.2
  31.7 490.9 %reduce-scatter.19.cloned.1.call-start = ((), (), s32[]{:S(2)}) async-start(), calls=%async_computation.15 | async-start | bytes 1327104
  31.8 84.9 %collective-permute-start.5 = (bf16[96,768]{1,0:T(8,128)(2,1)S(1)}, bf16[96,768]{1,0:T(8,128)(2,1)}, u32[]{:S(2)}, u32[]{:S(2)}) collective-permute-start(bf16[96,768]{1,0:T(8,128)(2,1)S(1)} %collective-permute-done.4), channel_id=1, source_target_pairs={{1,0},{2,1},{3,2},{4,3},{5,4},{6,5},{7,6},{0,7},{9,8},{10,9},{11,1... | collective-permute-start | bytes 442376 | tf_op jit(solution)/shard_map/ppermute | solution.py:29
  39.5 77.1 %copy-start.30 = (bf16[96,768]{1,0:T(8,128)(2,1)}, bf16[96,768]{1,0:T(8,128)(2,1)S(1)}, u32[]{:S(2)}) copy-start(bf16[96,768]{1,0:T(8,128)(2,1)S(1)} %collective-permute-done.2) | copy-start | bytes 442372
  39.5 77.2 %collective-permute-start.3 = (bf16[96,768]{1,0:T(8,128)(2,1)S(1)}, bf16[96,768]{1,0:T(8,128)(2,1)}, u32[]{:S(2)}, u32[]{:S(2)}) collective-permute-start(bf16[96,768]{1,0:T(8,128)(2,1)S(1)} %collective-permute-done.2), channel_id=1, source_target_pairs={{0,1},{1,2},{2,3},{3,4},{4,5},{5,6},{6,7},{7,0},{8,9},{9,10},{10,1... | collective-permute-start | bytes 442376 | tf_op jit(solution)/shard_map/ppermute | solution.py:26
  85.0 33.7 %copy-start.25 = (bf16[96,768]{1,0:T(8,128)(2,1)S(1)}, bf16[96,768]{1,0:T(8,128)(2,1)}, u32[]{:S(2)}) copy-start(bf16[96,768]{1,0:T(8,128)(2,1)} %param.26) | copy-start | bytes 442372
  87.7 255.5 %copy-start.40 = (f32[768]{0:T(1024)}, f32[768]{0:T(1024)S(1)}, u32[]{:S(2)}) copy-start(f32[768]{0:T(1024)S(1)} %convert_element_type.231) | copy-start | bytes 9220
  87.7 215.2 %copy-start.48 = (f32[768]{0:T(1024)}, f32[768]{0:T(1024)S(1)}, u32[]{:S(2)}) copy-start(f32[768]{0:T(1024)S(1)} %convert_element_type.232) | copy-start | bytes 9220
  116.7 7.1 copy-start.17
  116.7 5.4 collective-permute-start.6
  136.6 3.1 copy-start.18
  147.6 3.1 copy-start.33
  179.9 163.3 %copy-start.38 = (f32[1024]{0:T(1024)}, f32[1024]{0:T(1024)S(1)}, u32[]{:S(2)}) copy-start(f32[1024]{0:T(1024)S(1)} %broadcast_multiply_fusion.5) | copy-start | bytes 12292
  182.0 161.2 %copy-start.42 = (f32[1024]{0:T(1024)}, f32[1024]{0:T(1024)S(1)}, u32[]{:S(2)}) copy-start(f32[1024]{0:T(1024)S(1)} %add_rsqrt_fusion.1) | copy-start | bytes 12292
  223.2 79.8 %copy-start.50 = (f32[768]{0:T(1024)S(1)}, f32[768]{0:T(1024)}, u32[]{:S(2)}) copy-start(f32[768]{0:T(1024)} %convert_element_type.236) | copy-start | bytes 9220
  312.4 21.1 %copy-start = (f32[1024,768]{0,1:T(8,128)}, f32[1024,768]{0,1:T(8,128)S(1)}, u32[]{:S(2)}) copy-start(f32[1024,768]{0,1:T(8,128)S(1)} %get-tuple-element.304) | copy-start | bytes 9437188
  312.4 21.0 %copy-start.31 = (f32[1024]{0:T(1024)}, f32[1024]{0:T(1024)S(1)}, u32[]{:S(2)}) copy-start(f32[1024]{0:T(1024)S(1)} %broadcast_multiply_fusion.4) | copy-start | bytes 12292
  312.4 6.3 slice-start.2
  314.9 18.5 %copy-start.36 = (f32[1024]{0:T(1024)}, f32[1024]{0:T(1024)S(1)}, u32[]{:S(2)}) copy-start(f32[1024]{0:T(1024)S(1)} %add_rsqrt_fusion) | copy-start | bytes 12292
  314.9 3.8 slice-start.3
  316.9 16.6 %slice-start = ((s8[4718592]{0:T(1024)(128)(4,1)}), s8[4194304]{0:T(1024)(128)(4,1)S(1)}, s32[]{:S(2)}) async-start(s8[4718592]{0:T(1024)(128)(4,1)} %bitcast.217), calls=%async_computation.19 | async-start | bytes 8388608
  318.7 14.7 %copy-start.24 = (bf16[1024,768]{0,1:T(8,128)(2,1)}, bf16[1024,768]{0,1:T(8,128)(2,1)S(1)}, u32[]{:S(2)}) copy-start(bf16[1024,768]{0,1:T(8,128)(2,1)S(1)} %get-tuple-element.290) | copy-start | bytes 4718596
  318.7 14.7 %copy-start.8 = (f32[1024,768]{0,1:T(8,128)S(1)}, f32[1024,768]{0,1:T(8,128)}, u32[]{:S(2)}) copy-start(f32[1024,768]{0,1:T(8,128)} %copy-done.7) | copy-start | bytes 9437188
  318.7 14.7 %slice-start.1 = ((s8[4718592]{0:T(1024)(128)(4,1)}), s8[524288]{0:T(1024)(128)(4,1)S(1)}, s32[]{:S(2)}) async-start(s8[4718592]{0:T(1024)(128)(4,1)} %bitcast.217), calls=%async_computation.20 | async-start | bytes 1048576
  343.2 3.5 copy-start.54
  371.9 7.1 copy-start.14
  396.0 7.1 copy-start.14
  411.1 4.7 copy-start.19
  418.3 2.8 copy-start.16
  420.8 130.6 %reduce-scatter.21.cloned.1.call-start = ((), (), s32[]{:S(2)}) async-start(), calls=%async_computation.16 | async-start | bytes 1327104
  426.6 2.6 copy-start.6
  429.2 189.4 %reduce-scatter.23.cloned.1.call-start = ((), (), s32[]{:S(2)}) async-start(), calls=%async_computation.17 | async-start | bytes 1327104
  437.4 248.8 %reduce-scatter.13.cloned.1.call-start = ((), (), s32[]{:S(2)}) async-start(), calls=%async_computation.12 | async-start | bytes 1327104 | tf_op jit(solution)/shard_map/reduce_scatter | solution.py:275
  441.8 342.7 %reduce-scatter.17.cloned.1.call-start = ((), (), s32[]{:S(2)}) async-start(), calls=%async_computation.14 | async-start | bytes 5308416 | tf_op jit(solution)/shard_map/reduce_scatter | solution.py:211
  451.0 432.4 %reduce-scatter.15.cloned.1.call-start = ((), (), s32[]{:S(2)}) async-start(), calls=%async_computation.13 | async-start | bytes 5308416 | tf_op jit(solution)/shard_map/reduce_scatter | solution.py:205
  461.5 3.1 copy-start.55
  461.5 5.5 copy-start.44
  461.5 5.5 copy-start.45
  461.5 5.5 copy-start.46
  461.5 5.5 copy-start.47
  461.5 5.5 copy-start.51
  461.5 5.5 copy-start.52
  461.6 473.6 %all-reduce.23.cloned.1.call-start = ((), (), s32[]{:S(2)}) async-start(), calls=%async_computation.18 | async-start | bytes 3833856 | tf_op jit(solution)/shard_map/psum | solution.py:289
  463.2 50.1 %copy-start.22 = (bf16[96,8,2,512]{3,1,2,0:T(8,128)(2,1)S(1)}, bf16[96,8,2,512]{3,1,2,0:T(8,128)(2,1)}, u32[]{:S(2)}) copy-start(bf16[96,8,2,512]{3,1,2,0:T(8,128)(2,1)} %copy-done.21) | copy-start | bytes 4718596
  517.7 365.8 %copy-start.10 = (f32[1024,768]{0,1:T(8,128)S(1)}, f32[1024,768]{0,1:T(8,128)}, u32[]{:S(2)}) copy-start(f32[1024,768]{0,1:T(8,128)} %copy-done.9) | copy-start | bytes 9437188
  890.3 4.0 copy-start.1
  890.3 4.0 copy-start.32
  890.3 4.0 copy-start.35
  890.3 4.0 copy-start.37
  935.1 4.4 copy-start.29
  935.1 5.1 copy-start.28
  935.1 6.0 copy-start.27
  935.1 6.9 copy-start.26
  (21 other events, 35.4 us)
Sparse Core Ops, SparseCore 0:
  10.2 48.5 all-gather.7
  60.9 39.5 all-gather.9
  102.7 40.2 all-gather.11
  145.1 78.0 all-gather.13
  225.2 77.6 all-gather.15
  305.0 39.4 all-gather.17
  420.9 63.2 reduce-scatter.18
  487.6 63.7 reduce-scatter.20
  554.8 63.7 reduce-scatter.22
  622.4 63.7 reduce-scatter.12
  689.8 94.6 reduce-scatter.16
  788.0 95.3 reduce-scatter.14
  886.8 48.3 all-reduce.22
